TPU v7x, 32 devices: a whole 2x2x4 slice. The times are simulated.
32 devices in a mesh: row: 2 (over y), col: 4 (over x, core), layer: 4 (over z).
Axes of the slice: x: 2, y: 2, z: 4, core: 2. Of those that a mesh axis runs over, the one named last changes fastest.
Arguments:
- left: float32 [1024, 8192], P('row', ('layer', 'col')), may hold values from -6 to 6
- right: float32 [8192, 16384], P(('layer', 'row'), 'col'), may hold values from -0.125 to 0.125
- left_mask: int32 [2, 16], replicated, may hold values 0 or 1
- right_mask: int32 [16, 32], replicated, may hold values 0 or 1
- result_mask: int32 [2, 32], replicated, may hold values 0 or 1
Outputs:
- ladder: float32 [1024, 16384], P('row', ('col', 'layer'))
Inputs may be any that keep to these rules, and one draw needn't show every extreme that they name: `left_mask`: 1 marks a present tile, 0 an absent one. `right_mask`: 1 marks a present tile, 0 an absent one. `result_mask`: 1 marks a present tile, 0 an absent one.
All inputs are finite; a program needn't handle non-finite values.
Results may differ from a plain program's by a relative error of at most 0.0003.
Values sent between devices are 32-bit elements; how exact they have to be, the bound alone decides.
A program may use at most 128 MiB of HBM per device.

v0:
```python
import jax
import jax.numpy as jnp
from jax import lax
from jax.sharding import PartitionSpec as P

TILE = 512


def expand(table, row_start, rows, col_start, cols):
    row_ids = (row_start + jnp.arange(rows, dtype=jnp.int32)) // TILE
    col_ids = (col_start + jnp.arange(cols, dtype=jnp.int32)) // TILE
    row_sel = (row_ids[:, None] == jnp.arange(table.shape[0], dtype=jnp.int32)[None, :]).astype(
        jnp.float32
    )
    col_sel = (col_ids[:, None] == jnp.arange(table.shape[1], dtype=jnp.int32)[None, :]).astype(
        jnp.float32
    )
    inner = jnp.dot(row_sel, table.astype(jnp.float32), precision=lax.Precision.HIGHEST)
    return jnp.dot(inner, col_sel.T, precision=lax.Precision.HIGHEST)


def shards(left, right, left_mask, right_mask, result_mask):
    rows, left_cols = left.shape
    right_rows, right_cols = right.shape
    row_pos = lax.axis_index("row")
    col_pos = lax.axis_index("col")
    layer_pos = lax.axis_index("layer")
    col_count = lax.axis_size("col")
    row_count = lax.axis_size("row")
    layer_count = lax.axis_size("layer")
    left_start = (layer_pos * col_count + col_pos) * left_cols
    right_start = (layer_pos * row_count + row_pos) * right_rows
    left_used = left * expand(left_mask, row_pos * rows, rows, left_start, left_cols)
    right_used = right * expand(
        right_mask, right_start, right_rows, col_pos * right_cols, right_cols
    )
    out_cols = right_cols // layer_count
    slab = lax.all_gather(right_used, "row", axis=0, tiled=True)
    partial_sum = jnp.dot(
        lax.all_gather(left_used, "col", axis=1, tiled=True),
        slab,
        precision=lax.Precision.HIGHEST,
        preferred_element_type=jnp.float32,
    )
    product = lax.psum_scatter(partial_sum, "layer", scatter_dimension=1, tiled=True)
    keep = expand(
        result_mask, row_pos * rows, rows, (col_pos * layer_count + layer_pos) * out_cols, out_cols
    )
    return product * keep


def solution(mesh):
    placed = (P("row", ("layer", "col")), P(("layer", "row"), "col"), P(), P(), P())
    return jax.shard_map(
        shards, mesh=mesh, in_specs=placed, out_specs=P("row", ("col", "layer")), check_vma=False
    )
```

profile of v0, /device:TPU:0, one launch (start us, length us, event | category | flops | bytes accessed | tf_op | source)
XLA Modules:
  0.0 652.3 jit_solution(17251776173520304404)
XLA Ops:
  6.5 0.0 all-gather.3.cloned.1.call-start
  6.6 1.0 fusion.5
  7.6 2.9 convolution_multiply_fusion.2
  10.5 0.0 all-gather.3.cloned.1.call-update
  10.5 0.0 all-gather.5.cloned.1.call-start
  10.6 1.2 fusion
  11.8 13.7 %convolution_multiply_fusion = f32[1024,4096]{1,0:T(8,128)} fusion(f32[1024,4096]{1,0:T(8,128)} %param.6, f32[1024,32]{1,0:T(8,128)S(1)} %fusion, s32[4096]{0:T(1024)S(1)} %add_select_fusion), kind=kOutput, calls=%fused_computation | convolution fusion | flops 1614938112 | bytes 33701888 | tf_op jit(solution)/shard_map/dot_general | solution.py:19
  25.4 0.0 all-gather.5.cloned.1.call-update
  25.4 0.0 reduce-scatter.2.cloned.1.call-start
  25.5 22.3 %all-gather.3.cloned.1.call-done = f32[512,2048]{1,0:T(8,128)} async-done(((f32[512,512]{1,0:T(8,128)}), f32[512,2048]{1,0:T(8,128)}) %all-gather.3.cloned.1.call-update) | async-done | bytes 4194320 | tf_op jit(solution)/shard_map/all_gather | solution.py:40
  47.8 390.1 %all-gather.5.cloned.1.call-done = f32[2048,4096]{1,0:T(8,128)} async-done(((f32[1024,4096]{1,0:T(8,128)}), f32[2048,4096]{1,0:T(8,128)}) %all-gather.5.cloned.1.call-update) | async-done | bytes 33554448 | tf_op jit(solution)/shard_map/all_gather | solution.py:38
  438.0 59.0 %fusion.27 = f32[512,4096]{1,0:T(8,128)} fusion(f32[512,2048]{1,0:T(8,128)} %all-gather.3.cloned.1.call-done, f32[2048,4096]{1,0:T(8,128)} %all-gather.5.cloned.1.call-done), kind=kOutput, calls=%fused_computation.65 | convolution fusion | flops 51539607552 | bytes 46137344 | tf_op jit(solution)/shard_map/dot_general | solution.py:39
  496.9 0.0 copy-start
  496.9 0.0 reduce-scatter.2.cloned.1.call-update
  497.0 0.6 copy-done
  497.6 0.3 fusion.4
  497.9 143.8 %reduce-scatter.2.cloned.1.call-done = f32[512,1024]{1,0:T(8,128)} async-done(((f32[512,4096]{1,0:T(8,128)}), f32[512,1024]{1,0:T(8,128)}) %reduce-scatter.2.cloned.1.call-update) | async-done | bytes 2097168 | tf_op jit(solution)/shard_map/reduce_scatter | solution.py:45
  641.7 4.0 convolution_multiply_fusion.1
  (5 shorter events, 0.1 us)
Async XLA Ops:
  6.5 41.3 %all-gather.3.cloned.1.call-start = ((), (), s32[]{:S(2)}) async-start(), calls=%async_computation.1 | async-start | bytes 5242880 | tf_op jit(solution)/shard_map/all_gather | solution.py:40
  10.5 427.5 %all-gather.5.cloned.1.call-start = ((), (), s32[]{:S(2)}) async-start(), calls=%async_computation.2 | async-start | bytes 50331648 | tf_op jit(solution)/shard_map/all_gather | solution.py:38
  25.4 616.3 %reduce-scatter.2.cloned.1.call-start = ((), (), s32[]{:S(2)}) async-start(), calls=%async_computation.3 | async-start | bytes 10485760 | tf_op jit(solution)/shard_map/reduce_scatter | solution.py:45
  496.9 0.7 copy-start
Sparse Core Ops, SparseCore 0:
  10.6 37.1 all-gather.2
  49.4 388.5 all-gather.4
  497.1 144.6 reduce-scatter.1
where the time goes:
time: 653 us; the launch traced here: 652 us
  waiting for transfers between devices  556 us (85%)
  matrix products  82 us (13%)
  between operations  13.2 us (2%)
    all_gather x1, waiting for transfers between devices, shards(): slab = lax.all_gather(right_used, 'row', axis=0, tiled=True)  390 us
    reduce_scatter x1, waiting for transfers between devices, shards(): lax.psum_scatter(partial_sum, 'layer', scatter_dimension=1, tiled=True)  144 us
    dot_general x1, matrix products, shards(): jnp.dot(lax.all_gather(left_used, 'col', axis=1, tiled=True), slab, preci...  59 us
    all_gather x1, waiting for transfers between devices, shards(): lax.all_gather(left_used, 'col', axis=1, tiled=True)  22.3 us
    dot_general x3, matrix products, expand(): return jnp.dot(inner, col_sel.T, precision=lax.Precision.HIGHEST)  20.5 us
  transfers between devices with their start and end apart: 3, of which 3 were waited for; matrix products, arithmetic and copies ran while one was open for 2% of the time, Pallas kernels for 0%

commit v1 on v0

--- a/solution.py
+++ b/solution.py
@@ -1,9 +1,26 @@
+import functools
 import jax
 import jax.numpy as jnp
 from jax import lax
 from jax.sharding import PartitionSpec as P
+from jax.lax import axis_index, ppermute, psum
 
 TILE = 512
+
+
+def use_waves(block_here, chip_axis):
+    e_next, field_out = (psum(1, axis_name=chip_axis), axis_index(chip_axis))
+    built, tall = (block_here, 1)
+    while tall < e_next:
+        last = ppermute(built, axis_name=chip_axis, perm=[(j, j ^ tall) for j in range(e_next)])
+        spare = jnp.concatenate([built, last], axis=0)
+        block_out = jnp.concatenate([last, built], axis=0)
+        built = jnp.where(field_out & tall == 0, spare, block_out)
+        tall = 2 * tall
+    return built
+
+
+meet_pipes = functools.partial(use_waves, chip_axis="row")
 
 
 def expand(table, row_start, rows, col_start, cols):
@@ -35,7 +52,7 @@
         right_mask, right_start, right_rows, col_pos * right_cols, right_cols
     )
     out_cols = right_cols // layer_count
-    slab = lax.all_gather(right_used, "row", axis=0, tiled=True)
+    slab = meet_pipes(right_used)
     partial_sum = jnp.dot(
         lax.all_gather(left_used, "col", axis=1, tiled=True),
         slab,

time: 653 us -> 603 us (0.923)
  waiting for transfers between devices: 556 us -> 503 us
    all_gather x1 -> x0, waiting for transfers between devices: 390 us -> none  [shards(): slab = lax.all_gather(right_used, 'row', axis=0, tiled=True)]
    ppermute x0 -> x1, waiting for transfers between devices: none -> 324 us  [use_waves(): ppermute(built, axis_name=chip_axis, perm=[(j, j ^ tall) for j in range(e...]
    all_gather x1, waiting for transfers between devices: 22.3 us -> 34.6 us  [shards(): lax.all_gather(left_used, 'col', axis=1, tiled=True)]
  transfers between devices with their start and end apart: 3 -> 3, of which waited for: 3 -> 3; matrix products, arithmetic and copies ran while one was open for 2% -> 1% of each run, Pallas kernels for 0% -> 0%
where the time goes in v1:
time: 603 us
  waiting for transfers between devices  503 us (83%)
  matrix products  79.4 us (13%)
  between operations  13.5 us (2%)
    ppermute x1, waiting for transfers between devices, use_waves(): ppermute(built, axis_name=chip_axis, perm=[(j, j ^ tall) for j in range(e...  324 us
    reduce_scatter x1, waiting for transfers between devices, shards(): lax.psum_scatter(partial_sum, 'layer', scatter_dimension=1, tiled=True)  145 us
    dot_general x1, matrix products, shards(): jnp.dot(lax.all_gather(left_used, 'col', axis=1, tiled=True), slab, preci...  61.4 us
    all_gather x1, waiting for transfers between devices, shards(): lax.all_gather(left_used, 'col', axis=1, tiled=True)  34.6 us
    dot_general x3, matrix products, expand(): return jnp.dot(inner, col_sel.T, precision=lax.Precision.HIGHEST)  16.3 us
  transfers between devices with their start and end apart: 3, of which 3 were waited for; matrix products, arithmetic and copies ran while one was open for 1% of the time, Pallas kernels for 0%

profile of v1, /device:TPU:0, one launch (start us, length us, event | category | flops | bytes accessed | tf_op | source)
XLA Modules:
  0.0 602.6 jit_solution(3392135930649259974)
XLA Ops:
  6.5 0.0 all-gather.2.cloned.1.call-start
  6.6 1.2 fusion.7
  7.7 0.0 copy-start.1
  7.8 0.0 copy-start
  7.8 13.5 %convolution_multiply_fusion = f32[1024,4096]{1,0:T(8,128)} fusion(f32[1024,4096]{1,0:T(8,128)} %param.6, f32[1024,32]{1,0:T(8,128)S(1)} %fusion.7, s32[4096]{0:T(1024)S(1)} %add_select_fusion), kind=kOutput, calls=%fused_computation.8 | convolution fusion | flops 1614938112 | bytes 33701888 | tf_op jit(solution)/shard_map/dot_general | solution.py:36
  21.3 3.0 collective-permute-start
  24.3 0.0 copy-done.1
  24.3 0.3 fusion.13
  24.7 0.0 copy-done
  24.7 1.7 convolution_multiply_fusion.1
  26.3 0.0 all-gather.2.cloned.1.call-update
  26.4 0.2 reduce-scatter.2.cloned.1.call-start
  26.6 0.0 copy-start.2
  26.6 34.6 %all-gather.2.cloned.1.call-done = f32[512,2048]{1,0:T(8,128)} async-done(((f32[512,512]{1,0:T(8,128)}), f32[512,2048]{1,0:T(8,128)}) %all-gather.2.cloned.1.call-update) | async-done | bytes 4194320 | tf_op jit(solution)/shard_map/all_gather | solution.py:57
  61.3 323.5 %collective-permute-done = f32[1024,4096]{1,0:T(8,128)} collective-permute-done((f32[1024,4096]{1,0:T(8,128)}, f32[1024,4096]{1,0:T(8,128)}, u32[]{:S(2)}, u32[]{:S(2)}) %collective-permute-start) | collective-permute-done | bytes 16777248 | tf_op jit(solution)/shard_map/ppermute | solution.py:15
  384.8 61.4 %fusion = f32[512,4096]{1,0:T(8,128)} fusion(f32[512,2048]{1,0:T(8,128)} %all-gather.2.cloned.1.call-done, f32[1024,4096]{1,0:T(8,128)} %collective-permute-done, f32[1024,4096]{1,0:T(8,128)} %convolution_multiply_fusion, pred[]{:T(512)S(6)} %eq.38), kind=kOutput, calls=%fused_computation.1 | convolution fusion | flops 51564773376 | bytes 46137344 | tf_op jit(solution)/shard_map/dot_general | solution.py:56
  446.2 0.0 reduce-scatter.2.cloned.1.call-update
  446.2 0.0 copy-done.2
  446.2 0.3 fusion.12
  446.6 1.1 fusion.8
  447.6 144.8 %reduce-scatter.2.cloned.1.call-done = f32[512,1024]{1,0:T(8,128)} async-done(((f32[512,4096]{1,0:T(8,128)}), f32[512,1024]{1,0:T(8,128)}) %reduce-scatter.2.cloned.1.call-update) | async-done | bytes 2097168 | tf_op jit(solution)/shard_map/reduce_scatter | solution.py:62
  592.4 3.3 mul.44
  (5 shorter events, 0.1 us)
Async XLA Ops:
  6.5 54.7 %all-gather.2.cloned.1.call-start = ((), (), s32[]{:S(2)}) async-start(), calls=%async_computation.1 | async-start | bytes 5242880 | tf_op jit(solution)/shard_map/all_gather | solution.py:57
  7.7 16.6 %copy-start.1 = (s32[2,16]{1,0:T(2,128)S(1)}, s32[2,16]{1,0:T(2,128)}, u32[]{:S(2)}) copy-start(s32[2,16]{1,0:T(2,128)} %param.7) | copy-start | bytes 388
  7.8 16.9 %copy-start = (f32[512,512]{1,0:T(8,128)S(1)}, f32[512,512]{1,0:T(8,128)}, u32[]{:S(2)}) copy-start(f32[512,512]{1,0:T(8,128)} %param.5) | copy-start | bytes 3145732
  21.3 363.5 %collective-permute-start = (f32[1024,4096]{1,0:T(8,128)}, f32[1024,4096]{1,0:T(8,128)}, u32[]{:S(2)}, u32[]{:S(2)}) collective-permute-start(f32[1024,4096]{1,0:T(8,128)} %convolution_multiply_fusion), channel_id=1, source_target_pairs={{0,16},{16,0},{1,17},{17,1},{2,18},{18,2},{3,19},{19,3},{4,20},{20... | collective-permute-start | bytes 50331656 | tf_op jit(solution)/shard_map/ppermute | solution.py:15
  26.4 566.1 %reduce-scatter.2.cloned.1.call-start = ((), (), s32[]{:S(2)}) async-start(), calls=%async_computation.2 | async-start | bytes 10485760 | tf_op jit(solution)/shard_map/reduce_scatter | solution.py:62
  26.6 419.6 %copy-start.2 = (s32[2,32]{1,0:T(2,128)S(1)}, s32[2,32]{1,0:T(2,128)}, u32[]{:S(2)}) copy-start(s32[2,32]{1,0:T(2,128)} %param.9) | copy-start | bytes 772
Sparse Core Ops, SparseCore 0:
  26.5 34.7 all-gather.1
  446.3 146.0 reduce-scatter.1
